TPU v7x, 256 devices: a whole 4x4x8 slice. The times are simulated.
256 devices in a mesh: ctx: 16 (over z, x_hi), head: 16 (over x_lo, y, core).
Axes of the slice: x: 4 (x_hi: 2, x_lo: 2; x = x_hi * 2 + x_lo), y: 4, z: 8, core: 2. Of those that a mesh axis runs over, the one named last changes fastest.
Arguments:
- hidden: bfloat16 [16384, 8192], P('ctx', 'head'), may hold values from -6 to 6
- query_frozen_projection: bfloat16 [16384, 8192], P('ctx', 'head'), may hold values from -20 to 20
- key_projected: bfloat16 [16384, 1024], P('ctx'), may hold values from -20 to 20
- value_frozen_projection: bfloat16 [16384, 1024], P('ctx'), may hold values from -6 to 6
- query_down_factor: bfloat16 [8192, 16], P('head'), may hold values from -0.0625 to 0.0625
- query_up_factor: bfloat16 [16, 8192], P(None, 'head'), may hold values from -1.5 to 1.5
- value_down_factor: bfloat16 [8192, 16], P('head'), may hold values from -0.0625 to 0.0625
- value_up_factor: bfloat16 [16, 1024], replicated, may hold values from -1.5 to 1.5
- output_gradient: bfloat16 [16384, 8192], P('ctx', 'head'), may hold values from -0.046875 to 0.046875
- head_shift_mask: int32 [64], P('head'), may hold values from 0 to 1, as said below
Outputs:
- grad_a_q: float32 [8192, 16], P('head')
- query_up_gradient: float32 [16, 8192], P(None, 'head')
- grad_a_v: float32 [8192, 16], P('head')
- value_up_gradient: float32 [16, 1024], replicated
Inputs may be any that keep to these rules, and one draw needn't show every extreme that they name: `head_shift_mask`: exactly 32 of the heads carry 1.
All inputs are finite; a program needn't handle non-finite values.
Results may differ from a plain program's by a relative error of at most 0.0173.
The roundings to bfloat16 on the way count: a program that leaves them out, or rounds other values in their place, can miss the bound.
Values may be sent and summed in bfloat16 or wider, within the bound.
A program may use at most 128 MiB of HBM per device.

v0:
```python
import jax
import jax.numpy as jnp
from jax import lax
from jax.sharding import PartitionSpec as P

QUERY_HEADS = 64
KEY_VALUE_HEADS = 8
HEAD_SIZE = 128
adapter_scale = 2.0
pos_interp = 32.0
rope_base = 10000.0


def passed_along(block, axis, distance):
    devices = range(lax.axis_size(axis))
    route = [((i - distance) % len(devices), i) for i in devices]
    return lax.ppermute(block, axis, route)


def rope_tables(positions, head_width):
    half_width = head_width // 2
    inv_freq = rope_base ** (-(jnp.arange(half_width, dtype=jnp.float32) * 2.0 / head_width))
    angles = (positions.astype(jnp.float32) / pos_interp)[:, None] * inv_freq[None, :]
    return (jnp.cos(angles), jnp.sin(angles))


def rotate(tensor, cosine, sine_table):
    half_width = tensor.shape[-1] // 2
    first_half = tensor[..., :half_width]
    second_half = tensor[..., half_width:]
    return jnp.concatenate(
        [
            first_half * cosine - second_half * sine_table,
            second_half * cosine + first_half * sine_table,
        ],
        axis=-1,
    )


def unrotate(tensor, cosine, sine_table):
    half_width = tensor.shape[-1] // 2
    first_half = tensor[..., :half_width]
    second_half = tensor[..., half_width:]
    return jnp.concatenate(
        [
            first_half * cosine + second_half * sine_table,
            second_half * cosine - first_half * sine_table,
        ],
        axis=-1,
    )


def group_grads(query_rows, key_rows, value_rows, upstream):
    scale_factor = query_rows.shape[-1] ** (-0.5)
    scores = jnp.dot(query_rows, key_rows.T, preferred_element_type=jnp.float32) * scale_factor
    row_ids = lax.broadcasted_iota(jnp.int32, scores.shape, 0)
    col_ids = lax.broadcasted_iota(jnp.int32, scores.shape, 1)
    scores = jnp.where(col_ids <= row_ids, scores, -1e30)
    row_peak = jnp.max(scores, axis=1, keepdims=True)
    weights = jnp.exp(scores - row_peak)
    probs = weights / jnp.sum(weights, axis=1, keepdims=True)
    probs_low = probs.astype(jnp.bfloat16)
    output = jnp.dot(probs_low, value_rows, preferred_element_type=jnp.float32)
    delta = jnp.sum(upstream.astype(jnp.float32) * output, axis=1, keepdims=True)
    prob_grad = jnp.dot(upstream, value_rows.T, preferred_element_type=jnp.float32)
    score_grad = (probs * (prob_grad - delta)).astype(jnp.bfloat16)
    query_grad = jnp.dot(score_grad, key_rows, preferred_element_type=jnp.float32) * scale_factor
    value_gradient_total = jnp.dot(probs_low.T, upstream, preferred_element_type=jnp.float32)
    return (query_grad, value_gradient_total)


def regroup(own_rows, next_rows, head_mask):
    half_rows = next_rows.shape[0]
    shifted = jnp.concatenate([own_rows[half_rows:], next_rows], axis=0)
    return jnp.where(head_mask, shifted, own_rows)


def split_rows(gradient, head_mask, half_rows):
    lower_rows = gradient[:, :half_rows]
    upper_rows = gradient[:, half_rows:]
    own_part = jnp.where(
        head_mask, jnp.concatenate([jnp.zeros_like(lower_rows), lower_rows], axis=1), gradient
    )
    send_part = jnp.where(head_mask, upper_rows, jnp.zeros_like(upper_rows))
    return (own_part, send_part)


def on_device(
    hidden,
    query_frozen_projection,
    key_projected,
    value_frozen_projection,
    query_down_factor,
    query_up_factor,
    value_down_factor,
    value_up_factor,
    output_gradient,
    head_shift_mask,
):
    highest_precision = lax.Precision.HIGHEST
    group_rows = hidden.shape[0]
    half_rows = group_rows // 2
    heads_here = head_shift_mask.shape[0]
    adapter_rank_width = query_down_factor.shape[1]
    per_kv = QUERY_HEADS // KEY_VALUE_HEADS
    local_key_value_heads = max(1, heads_here // per_kv)
    fan_out = heads_here // local_key_value_heads
    ctx_number = lax.axis_index("ctx")
    head_number = lax.axis_index("head")
    first_key_value_head = head_number * heads_here // per_kv
    query_partial_sum = jnp.dot(hidden, query_down_factor, preferred_element_type=jnp.float32)
    value_partial_sum = jnp.dot(hidden, value_down_factor, preferred_element_type=jnp.float32)
    summed_q, summed_v = lax.psum((query_partial_sum, value_partial_sum), "head")
    query_upstream = summed_q.astype(jnp.bfloat16)
    value_upstream = summed_v.astype(jnp.bfloat16)
    own_pos = ctx_number * group_rows + jnp.arange(group_rows, dtype=jnp.int32)
    cosine, sine_table = rope_tables(own_pos, HEAD_SIZE)
    cos_rows = cosine[:, None, :]
    sin_rows = sine_table[:, None, :]
    query_before_rotary = query_frozen_projection.astype(jnp.float32) + adapter_scale * jnp.dot(
        query_upstream.astype(jnp.float32),
        query_up_factor.astype(jnp.float32),
        precision=highest_precision,
    )
    query_rows = rotate(
        query_before_rotary.reshape(group_rows, heads_here, HEAD_SIZE), cos_rows, sin_rows
    ).astype(jnp.bfloat16)
    key_cols = lax.dynamic_slice_in_dim(
        key_projected, first_key_value_head * HEAD_SIZE, local_key_value_heads * HEAD_SIZE, 1
    )
    key_rows = rotate(
        key_cols.astype(jnp.float32).reshape(group_rows, local_key_value_heads, HEAD_SIZE),
        cos_rows,
        sin_rows,
    ).astype(jnp.bfloat16)
    value_up_local = lax.dynamic_slice_in_dim(
        value_up_factor, first_key_value_head * HEAD_SIZE, local_key_value_heads * HEAD_SIZE, 1
    )
    value_columns = lax.dynamic_slice_in_dim(
        value_frozen_projection,
        first_key_value_head * HEAD_SIZE,
        local_key_value_heads * HEAD_SIZE,
        1,
    )
    value_before_adapter = value_columns.astype(jnp.float32) + adapter_scale * jnp.dot(
        value_upstream.astype(jnp.float32),
        value_up_local.astype(jnp.float32),
        precision=highest_precision,
    )
    value_rows = value_before_adapter.astype(jnp.bfloat16).reshape(
        group_rows, local_key_value_heads, HEAD_SIZE
    )
    upstream = output_gradient.reshape(group_rows, heads_here, HEAD_SIZE)
    head_flags = head_shift_mask > 0
    token_mask = head_flags[None, :, None]
    stack_mask = head_flags[:, None, None]
    next_query, next_keys, next_values, next_upstream = passed_along(
        (
            query_rows[:half_rows],
            key_rows[:half_rows],
            value_rows[:half_rows],
            upstream[:half_rows],
        ),
        "ctx",
        -1,
    )
    group_query = regroup(query_rows, next_query, token_mask)
    group_keys = regroup(
        jnp.repeat(key_rows, fan_out, axis=1), jnp.repeat(next_keys, fan_out, axis=1), token_mask
    )
    group_values = regroup(
        jnp.repeat(value_rows, fan_out, axis=1),
        jnp.repeat(next_values, fan_out, axis=1),
        token_mask,
    )
    group_upstream = regroup(upstream, next_upstream, token_mask)
    stacked = (
        jnp.moveaxis(group_query, 1, 0),
        jnp.moveaxis(group_keys, 1, 0),
        jnp.moveaxis(group_values, 1, 0),
        jnp.moveaxis(group_upstream, 1, 0),
    )
    query_grads, value_grads = lax.map(
        lambda members: group_grads(members[0], members[1], members[2], members[3]), stacked
    )
    own_query, send_query = split_rows(query_grads, stack_mask, half_rows)
    own_value, send_value = split_rows(value_grads, stack_mask, half_rows)
    own_value_kv = own_value.reshape(local_key_value_heads, fan_out, group_rows, HEAD_SIZE).sum(
        axis=1
    )
    send_value_kv = send_value.reshape(local_key_value_heads, fan_out, half_rows, HEAD_SIZE).sum(
        axis=1
    )
    back_query, back_value = passed_along((send_query, send_value_kv), "ctx", 1)
    own_query = own_query.at[:, :half_rows].add(back_query)
    own_value_kv = own_value_kv.at[:, :half_rows].add(back_value)
    prior_gradient = unrotate(jnp.moveaxis(own_query, 0, 1), cos_rows, sin_rows).reshape(
        group_rows, heads_here * HEAD_SIZE
    )
    value_token_rows = jnp.moveaxis(own_value_kv, 0, 1).reshape(
        group_rows, local_key_value_heads * HEAD_SIZE
    )
    query_up_gradient_piece = adapter_scale * jnp.dot(
        query_upstream.astype(jnp.float32).T, prior_gradient, precision=highest_precision
    )
    value_gradient_piece = adapter_scale * jnp.dot(
        value_upstream.astype(jnp.float32).T, value_token_rows, precision=highest_precision
    )
    token_query_piece = adapter_scale * jnp.dot(
        prior_gradient, query_up_factor.astype(jnp.float32).T, precision=highest_precision
    )
    token_value_piece = adapter_scale * jnp.dot(
        value_token_rows, value_up_local.astype(jnp.float32).T, precision=highest_precision
    )
    value_full = lax.dynamic_update_slice_in_dim(
        jnp.zeros((adapter_rank_width, KEY_VALUE_HEADS * HEAD_SIZE), jnp.float32),
        value_gradient_piece,
        first_key_value_head * HEAD_SIZE,
        1,
    )
    token_query_gradient, token_value_gradient = lax.psum(
        (token_query_piece, token_value_piece), "head"
    )
    a_q_part = jnp.dot(
        hidden.T, token_query_gradient.astype(jnp.bfloat16), preferred_element_type=jnp.float32
    )
    a_v_part = jnp.dot(
        hidden.T, token_value_gradient.astype(jnp.bfloat16), preferred_element_type=jnp.float32
    )
    grad_a_q, grad_a_v, query_up_gradient = lax.psum(
        (a_q_part, a_v_part, query_up_gradient_piece), "ctx"
    )
    value_up_gradient = lax.psum(value_full, ("ctx", "head"))
    return (grad_a_q, query_up_gradient, grad_a_v, value_up_gradient)


def solution(mesh):
    return jax.shard_map(
        on_device,
        mesh=mesh,
        in_specs=(
            P("ctx", "head"),
            P("ctx", "head"),
            P("ctx", None),
            P("ctx", None),
            P("head", None),
            P(None, "head"),
            P("head", None),
            P(),
            P("ctx", "head"),
            P("head"),
        ),
        out_specs=(P("head", None), P(None, "head"), P("head", None), P()),
        check_vma=False,
    )
```

profile of v0, /device:TPU:8, one launch (start us, length us, event | category | flops | bytes accessed | tf_op | source)
XLA Modules:
  0.0 588.5 jit_solution(2511384332108965878)
XLA Ops:
  8.4 2.4 fusion.51
  11.6 8.3 %collective-permute-start.1 = (bf16[512,1,128]{2,0,1:T(8,128)(2,1)}, bf16[512,1,128]{2,0,1:T(8,128)(2,1)}, u32[]{:S(2)}, u32[]{:S(2)}) collective-permute-start(bf16[512,1,128]{2,0,1:T(8,128)(2,1)} %pad_maximum_fusion.3), channel_id=1, source_target_pairs={{16,0},{32,16},{48,32},{64,48},{80,64},{96,80},{112,96},{128,112},... | collective-permute-start | bytes 393224 | tf_op jit(solution)/shard_map/ppermute | solution.py:17
  19.9 1.8 multiply_cosine_fusion.1
  23.0 52.5 %all-reduce.13 = (bf16[1024,16]{0,1:T(8,128)(2,1)S(1)}, bf16[1024,16]{0,1:T(8,128)(2,1)}) all-reduce(f32[1024,16]{0,1:T(8,128)S(1)} %fusion.72, f32[1024,16]{0,1:T(8,128)S(1)} %fusion.73), channel_id=1, replica_groups=mesh['ctx'=16,'head'=16] {'head'}, use_global_device_ids=true, to_apply=%region_0.1 | all-reduce | flops 32768 | bytes 196608 | tf_op jit(solution)/shard_map/psum | solution.py:113
  78.1 2.0 collective-permute-start
  82.6 2.0 collective-permute-start.2
  87.3 2.0 collective-permute-start.3
  89.3 1.8 copy.47
  93.7 1.8 pad_maximum_fusion.2
  95.5 1.8 copy.41
  101.9 2.0 collective-permute-done.3
  108.5 4.5 fusion.45
  113.1 45.1 %while.14 = (s32[]{:T(128)}, f32[4,1024,128]{1,2,0:T(8,128)}, f32[4,1024,128]{1,2,0:T(8,128)}, bf16[4,1024,128]{1,2,0:T(8,128)(2,1)}, bf16[4,1024,128]{1,2,0:T(8...) while((s32[]{:T(128)}, f32[4,1024,128]{1,2,0:T(8,128)}, ...), condition=%wide.region_6.7_spmd, body=%wide.region_2.6_spmd.sunk | while | flops 1373107200 | bytes 51430568 | solution.py:183
  113.1 1.8 fusion.111
  116.9 1.7 fusion.115
  119.3 4.0 fusion.114
  124.3 1.8 fusion.111
  128.1 1.7 fusion.115
  130.6 4.0 fusion.114
  135.6 1.8 fusion.111
  139.4 1.7 fusion.115
  141.9 4.0 fusion.114
  146.9 1.8 fusion.111
  150.6 1.7 fusion.115
  153.2 4.0 fusion.114
  158.2 3.8 select_reduce_fusion.1
  162.0 2.0 collective-permute-start.4
  164.8 10.0 %collective-permute-done.5 = f32[1,512,128]{1,2,0:T(8,128)S(1)} collective-permute-done((f32[1,512,128]{1,2,0:T(8,128)S(1)}, f32[1,512,128]{1,2,0:T(8,128)S(1)}, u32[]{:S(2)}, u32[]{:S(2)}) %collective-permute-start.5) | collective-permute-done | bytes 262176 | tf_op jit(solution)/shard_map/ppermute | solution.py:17
  178.4 13.2 %collective-permute-done.4 = f32[4,512,128]{1,2,0:T(8,128)} collective-permute-done((f32[4,512,128]{1,2,0:T(8,128)}, f32[4,512,128]{1,2,0:T(8,128)}, u32[]{:S(2)}, u32[]{:S(2)}) %collective-permute-start.4) | collective-permute-done | bytes 1048608 | tf_op jit(solution)/shard_map/ppermute | solution.py:17
  196.2 61.3 %all-reduce.14 = (bf16[1024,16]{0,1:T(8,128)(2,1)S(1)}, bf16[1024,16]{0,1:T(8,128)(2,1)S(1)}) all-reduce(f32[1024,16]{0,1:T(8,128)S(1)} %convolution_multiply_fusion.2, f32[1024,16]{0,1:T(8,128)S(1)} %convolution_multiply_fusion.3), channel_id=1, replica_groups=mesh['ctx'=16,'head'=16] {'head'}, use_global_device_ids=true, to_apply=%region_7.8 | all-reduce | flops 32768 | bytes 196608 | tf_op jit(solution)/shard_map/psum | solution.py:221
  259.3 158.1 %all-reduce.10.cloned.1.call-done = f32[16,1024]{1,0:T(8,128)} async-done(((f32[16,1024]{1,0:T(8,128)}), f32[16,1024]{1,0:T(8,128)}) %all-reduce.10.cloned.1.call-update) | async-done | bytes 65552 | tf_op jit(solution)/shard_map/psum | solution.py:233
  417.4 158.7 %all-reduce.12.cloned.1.call-done = (f32[512,16]{0,1:T(8,128)}, f32[16,512]{1,0:T(8,128)}, f32[512,16]{0,1:T(8,128)}) async-done(((f32[512,16]{0,1:T(8,128)}, f32[16,512]{1,0:T(8,128)}, f32[512,16]{0,1:T(8,128)}), (f32[512,16]{0,1:T(8,128)}, f32[16,512]{1,0:T(8,128)}, f32[512,16]{0,1:T(8,128)})) %all-reduce.12.cloned.1.call-update) | async-done | bytes 98320 | tf_op jit(solution)/shard_map/psum | solution.py:230
  (140 shorter events, 54.1 us)
Async XLA Ops:
  7.2 14.5 %copy-start = (bf16[1024,512]{1,0:T(8,128)(2,1)S(1)}, bf16[1024,512]{1,0:T(8,128)(2,1)}, u32[]{:S(2)}) copy-start(bf16[1024,512]{1,0:T(8,128)(2,1)} %param.16) | copy-start | bytes 3145732
  7.2 14.5 %copy-start.24 = (bf16[512,16]{0,1:T(8,128)(2,1)S(1)}, bf16[512,16]{0,1:T(8,128)(2,1)}, u32[]{:S(2)}) copy-start(bf16[512,16]{0,1:T(8,128)(2,1)} %param.20) | copy-start | bytes 49156
  7.2 410.2 %all-reduce.10.cloned.1.call-start = ((), (), s32[]{:S(2)}) async-start(), calls=%async_computation | async-start | bytes 131072 | tf_op jit(solution)/shard_map/psum | solution.py:233
  8.4 13.7 %copy-start.25 = (bf16[512,16]{0,1:T(8,128)(2,1)S(1)}, bf16[512,16]{0,1:T(8,128)(2,1)}, u32[]{:S(2)}) copy-start(bf16[512,16]{0,1:T(8,128)(2,1)} %param.22) | copy-start | bytes 49156
  10.8 11.3 %copy-start.5 = (bf16[1024,1,64]{2,0,1:T(8,128)(2,1)}, bf16[1024,1,64]{2,0,1:T(8,128)(2,1)S(1)}, u32[]{:S(2)}) copy-start(bf16[1024,1,64]{2,0,1:T(8,128)(2,1)S(1)} %get-tuple-element.118) | copy-start | bytes 393220
  10.8 11.7 %copy-start.15 = (bf16[1024,512]{1,0:T(8,128)(2,1)S(1)}, bf16[1024,512]{1,0:T(8,128)(2,1)}, u32[]{:S(2)}) copy-start(bf16[1024,512]{1,0:T(8,128)(2,1)} %param.17) | copy-start | bytes 3145732
  11.6 88.6 %collective-permute-start.1 = (bf16[512,1,128]{2,0,1:T(8,128)(2,1)}, bf16[512,1,128]{2,0,1:T(8,128)(2,1)}, u32[]{:S(2)}, u32[]{:S(2)}) collective-permute-start(bf16[512,1,128]{2,0,1:T(8,128)(2,1)} %pad_maximum_fusion.3), channel_id=1, source_target_pairs={{16,0},{32,16},{48,32},{64,48},{80,64},{96,80},{112,96},{128,112},... | collective-permute-start | bytes 393224 | tf_op jit(solution)/shard_map/ppermute | solution.py:17
  21.7 53.8 %copy-start.23 = (bf16[16,512]{1,0:T(8,128)(2,1)S(1)}, bf16[16,512]{1,0:T(8,128)(2,1)}, u32[]{:S(2)}) copy-start(bf16[16,512]{1,0:T(8,128)(2,1)} %param.21) | copy-start | bytes 49156
  78.1 6.5 %copy-start.21 = (bf16[1024,16]{0,1:T(8,128)(2,1)S(1)}, bf16[1024,16]{0,1:T(8,128)(2,1)}, u32[]{:S(2)}) copy-start(bf16[1024,16]{0,1:T(8,128)(2,1)} %get-tuple-element.99) | copy-start | bytes 98308
  78.1 27.4 %collective-permute-start = (bf16[512,4,128]{0,2,1:T(8,128)(2,1)}, bf16[512,4,128]{0,2,1:T(8,128)(2,1)}, u32[]{:S(2)}, u32[]{:S(2)}) collective-permute-start(bf16[512,4,128]{0,2,1:T(8,128)(2,1)} %get-tuple-element.116), channel_id=1, source_target_pairs={{16,0},{32,16},{48,32},{64,48},{80,64},{96,80},{112,96},{128,112},... | collective-permute-start | bytes 1572872 | tf_op jit(solution)/shard_map/ppermute | solution.py:17
  82.6 22.9 %collective-permute-start.2 = (bf16[512,4,128]{0,2,1:T(8,128)(2,1)}, bf16[512,4,128]{0,2,1:T(8,128)(2,1)}, u32[]{:S(2)}, u32[]{:S(2)}) collective-permute-start(bf16[512,4,128]{0,2,1:T(8,128)(2,1)} %bitcast.15), channel_id=1, source_target_pairs={{16,0},{32,16},{48,32},{64,48},{80,64},{96,80},{112,96},{128,112},... | collective-permute-start | bytes 1572872 | tf_op jit(solution)/shard_map/ppermute | solution.py:17
  87.3 16.6 %collective-permute-start.3 = (bf16[512,1,128]{2,0,1:T(8,128)(2,1)}, bf16[512,1,128]{2,0,1:T(8,128)(2,1)}, u32[]{:S(2)}, u32[]{:S(2)}) collective-permute-start(bf16[512,1,128]{2,0,1:T(8,128)(2,1)} %get-tuple-element.120), channel_id=1, source_target_pairs={{16,0},{32,16},{48,32},{64,48},{80,64},{96,80},{112,96},{128,112},... | collective-permute-start | bytes 393224 | tf_op jit(solution)/shard_map/ppermute | solution.py:17
  95.5 13.0 %copy-start.13 = (bf16[1024,128]{0,1:T(8,128)(2,1)S(1)}, bf16[1024,128]{0,1:T(8,128)(2,1)}, u32[]{:S(2)}) copy-start(bf16[1024,128]{0,1:T(8,128)(2,1)} %copy.47) | copy-start | bytes 786436
  105.5 3.0 copy-start.11
  105.5 3.0 copy-start.12
  105.5 3.0 copy-start.14
  105.5 3.0 copy-start.26
  113.1 45.1 %copy-start.27 = (pred[4]{0:T(512)(128)(4,1)S(1)}, pred[4]{0:T(512)(128)(4,1)}, u32[]{:S(2)}) copy-start(pred[4]{0:T(512)(128)(4,1)} %broadcast_compare_fusion) | copy-start | bytes 16
  114.9 3.7 copy-start.1
  114.9 2.0 copy-start.17
  126.1 3.7 copy-start.1
  126.1 2.0 copy-start.17
  137.4 3.7 copy-start.1
  148.7 3.7 copy-start.1
  158.2 5.8 copy-start.2
  158.2 5.8 copy-start.3
  162.0 12.8 %collective-permute-start.5 = (f32[1,512,128]{1,2,0:T(8,128)S(1)}, f32[1,512,128]{1,2,0:T(8,128)S(1)}, u32[]{:S(2)}, u32[]{:S(2)}) collective-permute-start(f32[1,512,128]{1,2,0:T(8,128)S(1)} %bitcast.125), channel_id=1, source_target_pairs={{240,0},{0,16},{16,32},{32,48},{48,64},{64,80},{80,96},{96,112},{1... | collective-permute-start | bytes 786440 | tf_op jit(solution)/shard_map/ppermute | solution.py:17
  162.0 29.6 %collective-permute-start.4 = (f32[4,512,128]{1,2,0:T(8,128)}, f32[4,512,128]{1,2,0:T(8,128)}, u32[]{:S(2)}, u32[]{:S(2)}) collective-permute-start(f32[4,512,128]{1,2,0:T(8,128)} %get-tuple-element.124), channel_id=1, source_target_pairs={{240,0},{0,16},{16,32},{32,48},{48,64},{64,80},{80,96},{96,112},{1... | collective-permute-start | bytes 3145736 | tf_op jit(solution)/shard_map/ppermute | solution.py:17
  164.0 11.6 %copy-start.22 = (bf16[1024,16]{0,1:T(8,128)(2,1)S(1)}, bf16[1024,16]{0,1:T(8,128)(2,1)}, u32[]{:S(2)}) copy-start(bf16[1024,16]{0,1:T(8,128)(2,1)} %get-tuple-element.99) | copy-start | bytes 98308
  175.7 17.5 %copy-start.7 = (f32[1024,64]{0,1:T(8,128)S(1)}, f32[1024,64]{0,1:T(8,128)}, u32[]{:S(2)}) copy-start(f32[1024,64]{0,1:T(8,128)} %get-tuple-element.121) | copy-start | bytes 786436
  176.7 399.4 %all-reduce.12.cloned.1.call-start = ((), (), s32[]{:S(2)}) async-start(), calls=%async_computation.1 | async-start | bytes 196608 | tf_op jit(solution)/shard_map/psum | solution.py:230
  177.0 16.2 %copy-start.9 = (f32[1024,64]{0,1:T(8,128)S(1)}, f32[1024,64]{0,1:T(8,128)}, u32[]{:S(2)}) copy-start(f32[1024,64]{0,1:T(8,128)} %get-tuple-element.122) | copy-start | bytes 786436
  (13 other events, 16.4 us)
Sparse Core Ops, SparseCore 0:
  176.8 240.5 all-reduce.9
  420.8 155.2 all-reduce.11
where the time goes:
time: 590 us; the launch traced here: 589 us
  waiting for transfers between devices  342 us (58%)
  blocking collectives  114 us (19%)
  matrix products  41.3 us (7%)
  local copies, waits for them, and re-layouts  34.7 us (6%)
  other arithmetic  25.5 us (4%)
  starting transfers between devices  16.6 us (3%)
  between operations  14.4 us (2%)
    psum x1, waiting for transfers between devices, on_device(): lax.psum((a_q_part, a_v_part, query_up_gradient_piece), 'ctx')  159 us
    psum x1, waiting for transfers between devices, on_device(): value_up_gradient = lax.psum(value_full, ('ctx', 'head'))  158 us
    psum x1, blocking collectives, on_device(): lax.psum((token_query_piece, token_value_piece), 'head')  61.3 us
    psum x1, blocking collectives, on_device(): lax.psum((query_partial_sum, value_partial_sum), 'head')  52.5 us
    ppermute x6, waiting for transfers between devices, passed_along(): return lax.ppermute(block, axis, route)  25.2 us
    ppermute x6, starting transfers between devices, passed_along(): return lax.ppermute(block, axis, route)  16.3 us
    dot_general x4, matrix products, group_grads(): jnp.dot(score_grad, key_rows, preferred_element_type=jnp.float32)  15.8 us
  transfers between devices with their start and end apart: 8, of which 5 were waited for; matrix products, arithmetic and copies ran while one was open for 6% of the time, Pallas kernels for 0%

commit v1 on v0

--- a/solution.py
+++ b/solution.py
@@ -230,7 +230,7 @@
     grad_a_q, grad_a_v, query_up_gradient = lax.psum(
         (a_q_part, a_v_part, query_up_gradient_piece), "ctx"
     )
-    value_up_gradient = lax.psum(value_full, ("ctx", "head"))
+    value_up_gradient = jnp.sum(lax.all_gather(value_full, ("ctx", "head")), axis=0)
     return (grad_a_q, query_up_gradient, grad_a_v, value_up_gradient)
 
 

time: 590 us -> 448 us (0.76)
  waiting for transfers between devices: 342 us -> 181 us
  matrix products: 41.3 us -> 55.3 us
    psum x1 -> x0, waiting for transfers between devices: 158 us -> none  [on_device(): value_up_gradient = lax.psum(value_full, ('ctx', 'head'))]
    psum x1, waiting for transfers between devices: 159 us -> 117 us  [on_device(): lax.psum((a_q_part, a_v_part, query_up_gradient_piece), 'ctx')]
    all_gather x0 -> x1, waiting for transfers between devices: none -> 35.9 us  [on_device(): lax.all_gather(value_full, ('ctx', 'head'))]
    dot_general x4, matrix products: 6.81 us -> 15.7 us  [group_grads(): jnp.dot(probs_low.T, upstream, preferred_element_type=jnp.float32)]
    reduce_sum x0 -> x1, other arithmetic: none -> 7.31 us  [on_device(): jnp.sum(lax.all_gather(value_full, ('ctx', 'head')), axis=0)]
  transfers between devices with their start and end apart: 8 -> 8, of which waited for: 5 -> 4; matrix products, arithmetic and copies ran while one was open for 6% -> 9% of each run, Pallas kernels for 0% -> 0%
where the time goes in v1:
time: 448 us; the launch traced here: 447 us
  waiting for transfers between devices  181 us (40%)
  blocking collectives  114 us (25%)
  matrix products  55.3 us (12%)
  local copies, waits for them, and re-layouts  33.9 us (8%)
  other arithmetic  30.6 us (7%)
  starting transfers between devices  16.3 us (4%)
  between operations  15.9 us (4%)
    psum x1, waiting for transfers between devices, on_device(): lax.psum((a_q_part, a_v_part, query_up_gradient_piece), 'ctx')  117 us
    psum x1, blocking collectives, on_device(): lax.psum((token_query_piece, token_value_piece), 'head')  60.8 us
    psum x1, blocking collectives, on_device(): lax.psum((query_partial_sum, value_partial_sum), 'head')  53.1 us
    all_gather x1, waiting for transfers between devices, on_device(): lax.all_gather(value_full, ('ctx', 'head'))  35.9 us
    ppermute x6, waiting for transfers between devices, passed_along(): return lax.ppermute(block, axis, route)  27.5 us
    ppermute x6, starting transfers between devices, passed_along(): return lax.ppermute(block, axis, route)  16.2 us
    dot_general x4, matrix products, group_grads(): jnp.dot(score_grad, key_rows, preferred_element_type=jnp.float32)  15.8 us
    dot_general x4, matrix products, group_grads(): jnp.dot(probs_low.T, upstream, preferred_element_type=jnp.float32)  15.7 us
  transfers between devices with their start and end apart: 8, of which 4 were waited for; matrix products, arithmetic and copies ran while one was open for 9% of the time, Pallas kernels for 0%

profile of v1, /device:TPU:8, one launch (start us, length us, event | category | flops | bytes accessed | tf_op | source)
XLA Modules:
  0.0 446.9 jit_solution(8621361392438261842)
XLA Ops:
  11.4 53.1 %all-reduce.10 = (bf16[1024,16]{0,1:T(8,128)(2,1)S(1)}, bf16[1024,16]{0,1:T(8,128)(2,1)S(1)}) all-reduce(f32[1024,16]{0,1:T(8,128)S(1)} %fusion.73, f32[1024,16]{0,1:T(8,128)S(1)} %fusion.74), channel_id=1, replica_groups=mesh['ctx'=16,'head'=16] {'head'}, use_global_device_ids=true, to_apply=%region_0.1 | all-reduce | flops 32768 | bytes 196608 | tf_op jit(solution)/shard_map/psum | solution.py:113
  66.6 8.0 %collective-permute-start.3 = (bf16[512,1,128]{2,0,1:T(8,128)(2,1)}, bf16[512,1,128]{2,0,1:T(8,128)(2,1)}, u32[]{:S(2)}, u32[]{:S(2)}) collective-permute-start(bf16[512,1,128]{2,0,1:T(8,128)(2,1)} %get-tuple-element.120), channel_id=1, source_target_pairs={{16,0},{32,16},{48,32},{64,48},{80,64},{96,80},{112,96},{128,112},... | collective-permute-start | bytes 393224 | tf_op jit(solution)/shard_map/ppermute | solution.py:17
  81.6 3.2 collective-permute-start
  85.7 2.4 fusion.52
  90.4 1.8 copy.47
  93.2 1.8 pad_maximum_fusion.2
  95.0 1.8 copy.41
  98.5 1.7 copy.39
  107.7 4.5 %fusion.46 = (bf16[4,1024,128]{1,2,0:T(8,128)(2,1)}, bf16[4,1024,128]{1,2,0:T(8,128)(2,1)}, bf16[4,1024,128]{1,2,0:T(8,128)(2,1)}, bf16[4,1024,128]{1,2,0:T(8,128)(2,1)}) fusion(bf16[512,4,128]{0,2,1:T(8,128)(2,1)S(1)} %reshape.270, bf16[512,4,128]{0,2,1:T(8,128)(2,1)S(1)} %reshape.269, pred[4]{0:T(512)(128)(4,1)S(1)} %copy-done.23, ...), kind=kLoop, calls=%fused_computation.65 | loop fusion | flops 12582912 | bytes 11010052 | tf_op jit(solution)/shard_map/transpose | solution.py:180
  112.2 57.7 %while.14 = (s32[]{:T(128)}, f32[4,1024,128]{1,2,0:T(8,128)}, f32[4,1024,128]{1,2,0:T(8,128)}, bf16[4,1024,128]{1,2,0:T(8,128)(2,1)}, bf16[4,1024,128]{1,2,0:T(8...) while((s32[]{:T(128)}, f32[4,1024,128]{1,2,0:T(8,128)}, ...), condition=%wide.region_6.7_spmd, body=%wide.region_2.6_spmd.sunk | while | flops 1373107200 | bytes 47235736 | solution.py:183
  112.2 1.8 fusion.112
  116.0 1.7 fusion.114
  117.7 4.0 fusion.115
  122.7 3.9 fusion.116
  126.6 1.8 fusion.112
  132.1 4.0 fusion.115
  137.2 3.9 fusion.116
  141.0 1.8 fusion.112
  144.8 1.7 fusion.114
  146.5 4.0 fusion.115
  151.6 3.9 fusion.116
  155.5 1.8 fusion.112
  160.9 4.0 fusion.115
  166.0 4.0 fusion.116
  169.9 3.8 select_reduce_fusion.1
  173.8 2.7 collective-permute-start.5
  177.3 6.5 %collective-permute-done.5 = f32[1,512,128]{1,2,0:T(8,128)S(1)} collective-permute-done((f32[1,512,128]{1,2,0:T(8,128)S(1)}, f32[1,512,128]{1,2,0:T(8,128)S(1)}, u32[]{:S(2)}, u32[]{:S(2)}) %collective-permute-start.5) | collective-permute-done | bytes 262176 | tf_op jit(solution)/shard_map/ppermute | solution.py:17
  187.8 21.0 %collective-permute-done.4 = f32[4,512,128]{1,2,0:T(8,128)S(1)} collective-permute-done((f32[4,512,128]{1,2,0:T(8,128)}, f32[4,512,128]{1,2,0:T(8,128)S(1)}, u32[]{:S(2)}, u32[]{:S(2)}) %collective-permute-start.4) | collective-permute-done | bytes 1048608 | tf_op jit(solution)/shard_map/ppermute | solution.py:17
  210.4 60.8 %all-reduce.11 = (bf16[1024,16]{0,1:T(8,128)(2,1)S(1)}, bf16[1024,16]{0,1:T(8,128)(2,1)S(1)}) all-reduce(f32[1024,16]{0,1:T(8,128)S(1)} %convolution_multiply_fusion.2, f32[1024,16]{0,1:T(8,128)S(1)} %convolution_multiply_fusion.3), channel_id=1, replica_groups=mesh['ctx'=16,'head'=16] {'head'}, use_global_device_ids=true, to_apply=%region_7.8 | all-reduce | flops 32768 | bytes 196608 | tf_op jit(solution)/shard_map/psum | solution.py:221
  274.6 35.9 %all-gather.2.cloned.1.call-done = f32[256,16,1024]{2,1,0:T(8,128)} async-done(((f32[1,16,1024]{2,1,0:T(8,128)}), f32[256,16,1024]{2,1,0:T(8,128)}) %all-gather.2.cloned.1.call-update) | async-done | bytes 16777232 | tf_op jit(solution)/shard_map/all_gather | solution.py:233
  310.6 7.3 %reduce_sum.50 = f32[16,1024]{1,0:T(8,128)} reduce(f32[256,16,1024]{2,1,0:T(8,128)} %all-gather.2.cloned.1.call-done, f32[]{:T(128)} %constant.108.clone.1), dimensions={0}, to_apply=%region_14.15 | reduce | flops 4177920 | bytes 16842756 | tf_op jit(solution)/shard_map/reduce_sum | solution.py:233
  317.9 117.4 %all-reduce.9.cloned.1.call-done = (f32[512,16]{0,1:T(8,128)}, f32[16,512]{1,0:T(8,128)}, f32[512,16]{0,1:T(8,128)}) async-done(((f32[512,16]{0,1:T(8,128)}, f32[16,512]{1,0:T(8,128)}, f32[512,16]{0,1:T(8,128)}), (f32[512,16]{0,1:T(8,128)}, f32[16,512]{1,0:T(8,128)}, f32[512,16]{0,1:T(8,128)})) %all-reduce.9.cloned.1.call-update) | async-done | bytes 98320 | tf_op jit(solution)/shard_map/psum | solution.py:230
  (128 shorter events, 55.0 us)
Async XLA Ops:
  8.0 66.6 %copy-start.15 = (bf16[1024,512]{1,0:T(8,128)(2,1)S(1)}, bf16[1024,512]{1,0:T(8,128)(2,1)}, u32[]{:S(2)}) copy-start(bf16[1024,512]{1,0:T(8,128)(2,1)} %param.24) | copy-start | bytes 3145732
  8.0 302.5 %all-gather.2.cloned.1.call-start = ((), (), s32[]{:S(2)}) async-start(), calls=%async_computation | async-start | bytes 16842752 | tf_op jit(solution)/shard_map/all_gather | solution.py:233
  64.5 2.1 copy-start.20
  64.5 15.1 %copy-start.18 = (bf16[1024,16]{0,1:T(8,128)(2,1)}, bf16[1024,16]{0,1:T(8,128)(2,1)S(1)}, u32[]{:S(2)}) copy-start(bf16[1024,16]{0,1:T(8,128)(2,1)S(1)} %get-tuple-element.98) | copy-start | bytes 98308
  66.6 34.8 %collective-permute-start.3 = (bf16[512,1,128]{2,0,1:T(8,128)(2,1)}, bf16[512,1,128]{2,0,1:T(8,128)(2,1)}, u32[]{:S(2)}, u32[]{:S(2)}) collective-permute-start(bf16[512,1,128]{2,0,1:T(8,128)(2,1)} %get-tuple-element.120), channel_id=1, source_target_pairs={{16,0},{32,16},{48,32},{64,48},{80,64},{96,80},{112,96},{128,112},... | collective-permute-start | bytes 393224 | tf_op jit(solution)/shard_map/ppermute | solution.py:17
  75.2 4.4 copy-start.22
  76.3 28.4 %collective-permute-start.2 = (bf16[512,4,128]{0,2,1:T(8,128)(2,1)}, bf16[512,4,128]{0,2,1:T(8,128)(2,1)}, u32[]{:S(2)}, u32[]{:S(2)}) collective-permute-start(bf16[512,4,128]{0,2,1:T(8,128)(2,1)} %bitcast.15), channel_id=1, source_target_pairs={{16,0},{32,16},{48,32},{64,48},{80,64},{96,80},{112,96},{128,112},... | collective-permute-start | bytes 1572872 | tf_op jit(solution)/shard_map/ppermute | solution.py:17
  81.6 23.1 %collective-permute-start = (bf16[512,4,128]{0,2,1:T(8,128)(2,1)}, bf16[512,4,128]{0,2,1:T(8,128)(2,1)}, u32[]{:S(2)}, u32[]{:S(2)}) collective-permute-start(bf16[512,4,128]{0,2,1:T(8,128)(2,1)} %get-tuple-element.116), channel_id=1, source_target_pairs={{16,0},{32,16},{48,32},{64,48},{80,64},{96,80},{112,96},{128,112},... | collective-permute-start | bytes 1572872 | tf_op jit(solution)/shard_map/ppermute | solution.py:17
  89.6 13.4 %collective-permute-start.1 = (bf16[512,1,128]{2,0,1:T(8,128)(2,1)}, bf16[512,1,128]{2,0,1:T(8,128)(2,1)}, u32[]{:S(2)}, u32[]{:S(2)}) collective-permute-start(bf16[512,1,128]{2,0,1:T(8,128)(2,1)} %pad_maximum_fusion.3), channel_id=1, source_target_pairs={{16,0},{32,16},{48,32},{64,48},{80,64},{96,80},{112,96},{128,112},... | collective-permute-start | bytes 393224 | tf_op jit(solution)/shard_map/ppermute | solution.py:17
  98.5 9.2 %copy-start.13 = (bf16[1024,128]{0,1:T(8,128)(2,1)S(1)}, bf16[1024,128]{0,1:T(8,128)(2,1)}, u32[]{:S(2)}) copy-start(bf16[1024,128]{0,1:T(8,128)(2,1)} %copy.47) | copy-start | bytes 786436
  104.7 3.0 copy-start.11
  104.7 3.0 copy-start.12
  104.7 3.0 copy-start.14
  104.7 3.0 copy-start.23
  112.2 57.7 %copy-start.24 = (pred[4]{0:T(512)(128)(4,1)S(1)}, pred[4]{0:T(512)(128)(4,1)}, u32[]{:S(2)}) copy-start(pred[4]{0:T(512)(128)(4,1)} %broadcast_compare_fusion) | copy-start | bytes 16
  114.0 1.9 copy-start.1
  114.0 2.0 copy-start.16
  128.4 1.9 copy-start.1
  128.4 2.0 copy-start.16
  142.8 1.9 copy-start.1
  142.8 2.0 copy-start.16
  157.2 1.9 copy-start.1
  157.3 2.0 copy-start.16
  169.9 6.6 %copy-start.2 = (f32[4,1024,128]{1,2,0:T(8,128)S(1)}, f32[4,1024,128]{1,2,0:T(8,128)}, u32[]{:S(2)}) copy-start(f32[4,1024,128]{1,2,0:T(8,128)} %get-tuple-element.66) | copy-start | bytes 6291460
  169.9 6.6 %copy-start.3 = (f32[4,1024,128]{1,2,0:T(8,128)S(1)}, f32[4,1024,128]{1,2,0:T(8,128)}, u32[]{:S(2)}) copy-start(f32[4,1024,128]{1,2,0:T(8,128)} %get-tuple-element.67) | copy-start | bytes 6291460
  173.8 10.0 %collective-permute-start.5 = (f32[1,512,128]{1,2,0:T(8,128)S(1)}, f32[1,512,128]{1,2,0:T(8,128)S(1)}, u32[]{:S(2)}, u32[]{:S(2)}) collective-permute-start(f32[1,512,128]{1,2,0:T(8,128)S(1)} %bitcast.129), channel_id=1, source_target_pairs={{240,0},{0,16},{16,32},{32,48},{48,64},{64,80},{80,96},{96,112},{1... | collective-permute-start | bytes 786440 | tf_op jit(solution)/shard_map/ppermute | solution.py:17
  176.5 8.1 %copy-start.21 = (bf16[1024,16]{0,1:T(8,128)(2,1)S(1)}, bf16[1024,16]{0,1:T(8,128)(2,1)}, u32[]{:S(2)}) copy-start(bf16[1024,16]{0,1:T(8,128)(2,1)} %copy-done.20) | copy-start | bytes 98308
  184.7 24.4 %copy-start.7 = (f32[1024,64]{0,1:T(8,128)S(1)}, f32[1024,64]{0,1:T(8,128)}, u32[]{:S(2)}) copy-start(f32[1024,64]{0,1:T(8,128)} %copy-done.6) | copy-start | bytes 786436
  185.7 249.6 %all-reduce.9.cloned.1.call-start = ((), (), s32[]{:S(2)}) async-start(), calls=%async_computation.1 | async-start | bytes 196608 | tf_op jit(solution)/shard_map/psum | solution.py:230
  185.7 23.4 %copy-start.9 = (f32[1024,64]{0,1:T(8,128)S(1)}, f32[1024,64]{0,1:T(8,128)}, u32[]{:S(2)}) copy-start(f32[1024,64]{0,1:T(8,128)} %copy-done.8) | copy-start | bytes 786436
  185.7 23.1 %collective-permute-start.4 = (f32[4,512,128]{1,2,0:T(8,128)}, f32[4,512,128]{1,2,0:T(8,128)S(1)}, u32[]{:S(2)}, u32[]{:S(2)}) collective-permute-start(f32[4,512,128]{1,2,0:T(8,128)} %get-tuple-element.124), channel_id=1, source_target_pairs={{240,0},{0,16},{16,32},{32,48},{48,64},{64,80},{80,96},{96,112},{1... | collective-permute-start | bytes 3145736 | tf_op jit(solution)/shard_map/ppermute | solution.py:17
  209.6 63.3 %copy-start.19 = (bf16[1024,16]{0,1:T(8,128)(2,1)S(1)}, bf16[1024,16]{0,1:T(8,128)(2,1)}, u32[]{:S(2)}) copy-start(bf16[1024,16]{0,1:T(8,128)(2,1)} %copy-done.18) | copy-start | bytes 98308
  (7 other events, 6.0 us)
Sparse Core Ops, SparseCore 0:
  185.8 124.7 all-gather.1
Sparse Core Ops, SparseCore 1:
  274.7 160.5 all-reduce.8
